TPU v7x, 32 devices: a whole 2x2x4 slice. The times are simulated.
32 devices in a mesh: field: 8 (over y, x, core), point: 4 (over z).
Axes of the slice: x: 2, y: 2, z: 4, core: 2. Of those that a mesh axis runs over, the one named last changes fastest.
Arguments:
- residual_in: bfloat16 [8, 1024, 2048], P('field', 'point'), may hold values from -6 to 6
- coefs_in: bfloat16 [8, 1024, 4, 256], P('field', 'point'), may hold values from 0 to 1
- dictionary: bfloat16 [2048, 2048], P('field'), may hold values from -0.125 to 0.125
- owner_order: int32 [8], replicated, may hold values from 0 to 7, each once
- pixel_of: int32 [8, 1024], P('field', 'point'), may hold values from 0 to 1023, each once within a row
Outputs:
- maps: float32 [8, 4, 256, 8, 128], P('field', None, 'point')
Inputs may be any that keep to these rules, and one draw needn't show every extreme that they name: `owner_order`: A permutation of the dictionary blocks. `pixel_of`: each field's row is a permutation of its scan points over the 8 x 128 pixels.
All inputs are finite; a program needn't handle non-finite values.
Results may differ from a plain program's by a relative error of at most 0.00045.
Values may be sent and summed in bfloat16 or wider, within the bound.
No kernel may reach another device: no remote copies, remote signals or barrier semaphores. Data moves between devices by JAX's collectives and lax.ppermute only.
A program may use at most 64 MiB of HBM per device.

v0:
```python
import jax
import jax.numpy as jnp
from jax import lax
from jax.sharding import PartitionSpec as P

TURNS = 4
SWEEPS = 4
MAP_W = 128
time_step = 0.2
edge_scale = 0.5


def from_root(value, axis, source):
    kept = jnp.where(lax.axis_index(axis) == source, value, 0).astype(value.dtype)
    return lax.psum(kept, axis)


def block_steps(templates):
    gram = lax.dot_general(
        templates, templates, (((1,), (1,)), ((), ())), preferred_element_type=jnp.float32
    )
    return 1.0 / jnp.sum(jnp.abs(gram), axis=1)


def diffuse(grids):
    for repeat in range(SWEEPS):
        padded = jnp.pad(grids, ((0, 0), (1, 1), (1, 1)), mode="edge")
        summed = jnp.zeros_like(grids)
        for neighbour in (
            padded[:, :-2, 1:-1],
            padded[:, 2:, 1:-1],
            padded[:, 1:-1, :-2],
            padded[:, 1:-1, 2:],
        ):
            differ = neighbour - grids
            scaled = differ / edge_scale
            summed = summed + differ / (1.0 + scaled * scaled)
        grids = grids + time_step * summed
    return grids


def build_maps(moved, pixel_ids):
    points = moved.shape[0]
    count = moved.shape[1]
    local_kb = moved.shape[2]
    values = moved.reshape(points, count * local_kb).T
    flat = jnp.zeros((count * local_kb, points), jnp.float32).at[:, pixel_ids].set(values)
    grids = diffuse(flat.reshape(count * local_kb, points // MAP_W, MAP_W))
    return grids.reshape(count, local_kb, points // MAP_W, MAP_W)


def per_device(residual_in, coefs_in, dictionary, owner_order, pixel_of):
    residual = residual_in[0]
    coefs = coefs_in[0].astype(jnp.float32)
    pixel_ids = lax.all_gather(pixel_of[0], "point", axis=0, tiled=True)
    own_steps = block_steps(dictionary)
    updated = []
    for turn_index in range(TURNS):
        owner = owner_order[turn_index]
        templates = from_root(dictionary, "field", owner)
        step_size = from_root(own_steps, "field", owner)
        correlation = lax.dot_general(
            residual, templates, (((1,), (1,)), ((), ())), preferred_element_type=jnp.float32
        )
        before = coefs[:, turn_index, :]
        after = jnp.maximum(before + step_size[None, :] * correlation, 0.0)
        updated.append(after)
        if turn_index + 1 < TURNS:
            change = (after - before).astype(jnp.bfloat16)
            residual = (
                residual.astype(jnp.float32)
                - jnp.dot(change, templates, preferred_element_type=jnp.float32)
            ).astype(jnp.bfloat16)
    stacked = jnp.stack(updated, axis=1)
    maps = build_maps(
        lax.all_to_all(stacked, "point", split_axis=2, concat_axis=0, tiled=True), pixel_ids
    )
    return maps[None]


def solution(mesh):
    placed = (
        P("field", "point", None),
        P("field", "point", None, None),
        P("field", None),
        P(),
        P("field", "point"),
    )
    return jax.shard_map(
        per_device,
        mesh=mesh,
        in_specs=placed,
        out_specs=P("field", None, "point", None, None),
        check_vma=False,
    )
```

profile of v0, /device:TPU:0, one launch (start us, length us, event | category | flops | bytes accessed | tf_op | source)
XLA Modules:
  0.0 157.1 jit_solution(16890992155468359398)
XLA Ops:
  6.5 0.0 all-reduce.4.cloned.1.call-start
  6.5 1.4 fusion.65
  10.4 3.3 %broadcast_select_fusion.3 = (bf16[256,2048]{1,0:T(8,128)(2,1)}, bf16[256,2048]{1,0:T(8,128)(2,1)}, bf16[256,2048]{1,0:T(8,128)(2,1)}, bf16[256,2048]{1,0:T(8,128)(2,1)}) fusion(bf16[256,2048]{1,0:T(8,128)(2,1)} %param.7, pred[]{:T(512)S(6)} %eq.16, pred[]{:T(512)S(6)} %eq.17, pred[]{:T(512)S(6)} %eq.19, pred[]{:T(512)S(6)} %eq.18), kind=kLoop, calls=%fused_computation.117 | loop fusion | flops 2097152 | bytes 5242884 | tf_op jit(solution)/shard_map/jit(_where)/select_n | solution.py:14
  13.8 0.0 copy-start.5
  13.8 0.0 all-reduce.4.cloned.1.call-update
  13.8 1.0 copy-done.5
  14.8 0.0 copy-start.3
  14.8 0.3 copy.19
  15.1 0.9 copy-done.3
  16.0 0.5 fusion.15
  16.5 0.0 copy-start
  16.6 16.0 %all-reduce = (f32[256]{0:T(256)S(1)}, f32[256]{0:T(256)S(1)}, f32[256]{0:T(256)S(1)}, f32[256]{0:T(256)S(1)}) all-reduce(f32[256]{0:T(256)S(1)} %get-tuple-element.29, f32[256]{0:T(256)S(1)} %get-tuple-element.28, f32[256]{0:T(256)S(1)} %get-tuple-element.27, ...), channel_id=1, replica_groups=mesh['field'=8,'point'=4] {'field'}, use_global_device_ids=true, to_apply=%region_1.2 | all-reduce | flops 1024 | bytes 8192 | tf_op jit(solution)/shard_map/psum | solution.py:15
  32.5 0.1 bitcast_convert_fusion
  32.6 65.1 %all-reduce.4.cloned.1.call-done = (bf16[256,2048]{1,0:T(8,128)(2,1)}, bf16[256,2048]{1,0:T(8,128)(2,1)}, bf16[256,2048]{1,0:T(8,128)(2,1)}, bf16[256,2048]{1,0:T(8,128)(2,1)}) async-done(((bf16[256,2048]{1,0:T(8,128)(2,1)}, bf16[256,2048]{1,0:T(8,128)(2,1)}, bf16[256,2048]{1,0:T(8,128)(2,1)}, bf16[256,2048]{1,0:T(8,128)(2,1)}), (bf16[256,2048]{1,0:T(8,128)(2,1)}, bf16[256,2048]{1,0:T(8,128)(2,1)}, ...) | async-done | bytes 4194320 | tf_op jit(solution)/shard_map/psum | solution.py:15
  97.7 0.0 copy-done
  97.7 0.0 copy-start.2
  97.7 1.8 %fusion.14 = f32[256,256]{0,1:T(8,128)S(1)} fusion(bf16[256,2048]{1,0:T(8,128)(2,1)} %get-tuple-element.12, bf16[1,256,2048]{2,1,0:T(8,128)(2,1)S(1)} %copy-done, f32[256,4,256]{0,2,1:T(8,128)S(1)} %bitcast_convert_fusion, f32[256]{0:T(256)S(1)} %get-tuple-element.5), kind=kOutput, calls=%fused_computation.37 | convolution fusion | flops 268632064 | bytes 2622464 | tf_op jit(solution)/shard_map/dot_general | solution.py:62
  99.5 0.0 copy-done.2
  99.5 0.0 copy-start.1
  99.6 0.5 fusion
  100.0 0.7 copy-done.1
  100.8 0.5 fusion.11
  101.2 0.0 copy-start.4
  101.3 0.5 fusion.1
  101.7 0.7 copy-done.4
  102.5 0.5 fusion.9
  103.0 2.5 %fusion.7 = f32[256,1,256]{0,2,1:T(8,128)S(1)} fusion(bf16[256,2048]{1,0:T(8,128)(2,1)} %get-tuple-element.9, bf16[256,2048]{1,0:T(8,128)(2,1)} %get-tuple-element.10, bf16[256,2048]{1,0:T(8,128)(2,1)S(1)} %fusion.1, f32[256,4,256]{0,2,1:T(8,128)S(1)} %bitcast_convert_fusion, f32[256,256]{0,1:T(8,128)S(1)} %fusion.9, f32[256]{0:T(256)S(1)} %get-tuple-element.8), kind=kOutput, calls=%fused_computation.27 | convolution fusion | flops 538771456 | bytes 4195328 | tf_op jit(solution)/shard_map/dot_general | solution.py:62
  105.4 0.1 pad_maximum_fusion.24
  105.5 1.6 %copy.23 = f32[256,4,256]{0,1,2:T(4,128)} copy(f32[256,4,256]{0,2,1:T(8,128)S(1)} %pad_maximum_fusion.24) | data formatting | bytes 2097152 | tf_op jit(solution)/shard_map/stack | solution.py:74
  107.2 0.0 copy-start.6
  107.2 4.7 %all-to-all-start = ((f32[256,4,256]{0,1,2:T(4,128)}), f32[256,4,256]{0,1,2:T(4,128)S(1)}, u32[]{:S(2)}, u32[]{:S(2)}) async-start(f32[256,4,256]{0,1,2:T(4,128)} %copy.23), calls=%async_computation | async-start | bytes 2097152 | tf_op jit(solution)/shard_map/all_to_all | solution.py:76
  111.9 0.0 copy-done.6
  111.9 22.7 %all-gather = s32[1,1024]{1,0:T(1,128)S(1)} all-gather(s32[1,256]{1,0:T(1,128)S(1)} %copy-done.6), channel_id=2, replica_groups=mesh['field'=8,'point'=4] {'point'}, dimensions={1}, use_global_device_ids=true | all-gather | bytes 5120 | tf_op jit(solution)/shard_map/all_gather | solution.py:55
  134.6 2.8 %all-to-all-done = f32[256,4,256]{0,1,2:T(4,128)S(1)} async-done(((f32[256,4,256]{0,1,2:T(4,128)}), f32[256,4,256]{0,1,2:T(4,128)S(1)}, u32[]{:S(2)}, u32[]{:S(2)}) %all-to-all-start) | async-done | bytes 1048608 | tf_op jit(solution)/shard_map/all_to_all | solution.py:76
  137.5 0.7 copy.24
  138.1 0.2 copy.30
  138.3 0.3 copy.25
  138.7 5.0 %scatter_custom_fusion = f32[256,1024]{0,1:T(8,128)S(1)} fusion(s32[1024]{0:T(1024)S(1)} %compare_select_fusion, f32[1024,256]{1,0:T(8,128)S(1)} %copy.25, f32[]{:T(128)} %constant.32.clone.1), kind=kCustom, calls=%fused_computation.119 | custom fusion | bytes 1048580 | tf_op jit(solution)/shard_map/scatter | solution.py:47
  143.8 1.3 multiply_add_fusion.3
  145.1 1.3 multiply_add_fusion.2
  146.4 1.3 multiply_add_fusion.1
  147.7 1.3 multiply_add_fusion
  149.0 1.3 copy.26
  (7 shorter events, 0.1 us)
Async XLA Ops:
  6.5 91.2 %all-reduce.4.cloned.1.call-start = ((), (), s32[]{:S(2)}) async-start(), calls=%async_computation.1 | async-start | bytes 8388608 | tf_op jit(solution)/shard_map/psum | solution.py:15
  13.8 1.0 copy-start.5
  14.8 1.2 copy-start.3
  16.5 81.2 %copy-start = (bf16[1,256,2048]{2,1,0:T(8,128)(2,1)S(1)}, bf16[1,256,2048]{2,1,0:T(8,128)(2,1)}, u32[]{:S(2)}) copy-start(bf16[1,256,2048]{2,1,0:T(8,128)(2,1)} %param.5) | copy-start | bytes 3145732
  97.7 1.8 %copy-start.2 = (bf16[256,2048]{1,0:T(8,128)(2,1)S(1)}, bf16[256,2048]{1,0:T(8,128)(2,1)}, u32[]{:S(2)}) copy-start(bf16[256,2048]{1,0:T(8,128)(2,1)} %get-tuple-element.12) | copy-start | bytes 3145732
  99.5 1.2 copy-start.1
  101.2 1.2 copy-start.4
  107.2 4.7 %copy-start.6 = (s32[1,256]{1,0:T(1,128)S(1)}, s32[1,256]{1,0:T(1,128)}, u32[]{:S(2)}) copy-start(s32[1,256]{1,0:T(1,128)} %param.9) | copy-start | bytes 3076
  107.2 30.3 %all-to-all-start = ((f32[256,4,256]{0,1,2:T(4,128)}), f32[256,4,256]{0,1,2:T(4,128)S(1)}, u32[]{:S(2)}, u32[]{:S(2)}) async-start(f32[256,4,256]{0,1,2:T(4,128)} %copy.23), calls=%async_computation | async-start | bytes 2097152 | tf_op jit(solution)/shard_map/all_to_all | solution.py:76
Sparse Core Ops, SparseCore 0:
  13.9 83.7 all-reduce.3
where the time goes:
time: 158 us; the launch traced here: 157 us
  waiting for transfers between devices  67.9 us (43%)
  blocking collectives  38.7 us (24%)
  between operations  16.1 us (10%)
  local copies, waits for them, and re-layouts  14.5 us (9%)
  other arithmetic  8.6 us (5%)
  matrix products  6.61 us (4%)
  starting transfers between devices  4.74 us (3%)
    psum x1, waiting for transfers between devices, from_root(): return lax.psum(kept, axis)  65.1 us
    all_gather x1, blocking collectives, per_device(): pixel_ids = lax.all_gather(pixel_of[0], 'point', axis=0, tiled=True)  22.7 us
    psum x1, blocking collectives, from_root(): return lax.psum(kept, axis)  16 us
    dot_general x4, matrix products, per_device(): lax.dot_general(residual, templates, (((1,), (1,)), ((), ())), preferred_...  5.2 us
    add x4, other arithmetic, diffuse(): grids = grids + time_step * summed  5.1 us
    scatter x1, local copies, waits for them, and re-layouts, build_maps(): jnp.zeros((count * local_kb, points), jnp.float32).at[:, pixel_ids]  5.05 us
    all_to_all x1, starting transfers between devices, per_device(): lax.all_to_all(stacked, 'point', split_axis=2, concat_axis=0, tiled=True)  4.74 us
    unnamed x16, local copies, waits for them, and re-layouts  3.94 us
  transfers between devices with their start and end apart: 2, of which 2 were waited for; matrix products, arithmetic and copies ran while one was open for 1% of the time, Pallas kernels for 0%

commit v1 on v0

--- a/solution.py
+++ b/solution.py
@@ -52,7 +52,15 @@
 def per_device(residual_in, coefs_in, dictionary, owner_order, pixel_of):
     residual = residual_in[0]
     coefs = coefs_in[0].astype(jnp.float32)
-    pixel_ids = lax.all_gather(pixel_of[0], "point", axis=0, tiled=True)
+    own = pixel_of[0]
+    n_dev = lax.axis_size("point")
+    right = [(i, (i + 1) % n_dev) for i in range(n_dev)]
+    parts = [own]
+    for hop in range(1, n_dev):
+        parts = [lax.ppermute(parts[0], "point", right), *parts]
+    whole = jnp.concatenate(parts, axis=0)
+    turn = (lax.axis_index("point") + 1) * parts[-1].shape[0]
+    pixel_ids = jnp.roll(whole, turn, axis=0)
     own_steps = block_steps(dictionary)
     updated = []
     for turn_index in range(TURNS):

time: 158 us -> 164 us (1.038)
  blocking collectives: 38.7 us -> 16 us
  waiting for transfers between devices: 67.9 us -> 89.8 us
  starting transfers between devices: 4.74 us -> 11.7 us
    ppermute x0 -> x3, waiting for transfers between devices: none -> 24.7 us  [per_device(): parts = [lax.ppermute(parts[0], 'point', right), *parts]]
    all_gather x1 -> x0, blocking collectives: 22.7 us -> none  [per_device(): pixel_ids = lax.all_gather(pixel_of[0], 'point', axis=0, tiled=True)]
    ppermute x0 -> x3, starting transfers between devices: none -> 6.97 us  [per_device(): parts = [lax.ppermute(parts[0], 'point', right), *parts]]
    all_to_all x1, waiting for transfers between devices: 2.82 us -> 0.01 us  [per_device(): lax.all_to_all(stacked, 'point', split_axis=2, concat_axis=0, tiled=True)]
    unnamed x16 -> x23, local copies, waits for them, and re-layouts: 3.94 us -> 3.99 us
  transfers between devices with their start and end apart: 2 -> 5, of which waited for: 2 -> 4; matrix products, arithmetic and copies ran while one was open for 1% -> 1% of each run, Pallas kernels for 0% -> 0%
where the time goes in v1:
time: 164 us
  waiting for transfers between devices  89.8 us (55%)
  between operations  16.1 us (10%)
  blocking collectives  16 us (10%)
  local copies, waits for them, and re-layouts  14.7 us (9%)
  starting transfers between devices  11.7 us (7%)
  other arithmetic  8.69 us (5%)
  matrix products  6.61 us (4%)
    psum x1, waiting for transfers between devices, from_root(): return lax.psum(kept, axis)  65.1 us
    ppermute x3, waiting for transfers between devices, per_device(): parts = [lax.ppermute(parts[0], 'point', right), *parts]  24.7 us
    psum x1, blocking collectives, from_root(): return lax.psum(kept, axis)  16 us
    ppermute x3, starting transfers between devices, per_device(): parts = [lax.ppermute(parts[0], 'point', right), *parts]  6.97 us
    scatter x1, local copies, waits for them, and re-layouts, build_maps(): jnp.zeros((count * local_kb, points), jnp.float32).at[:, pixel_ids]  5.23 us
    dot_general x4, matrix products, per_device(): lax.dot_general(residual, templates, (((1,), (1,)), ((), ())), preferred_...  5.2 us
    add x4, other arithmetic, diffuse(): grids = grids + time_step * summed  5.09 us
    all_to_all x1, starting transfers between devices, per_device(): lax.all_to_all(stacked, 'point', split_axis=2, concat_axis=0, tiled=True)  4.74 us
  transfers between devices with their start and end apart: 5, of which 4 were waited for; matrix products, arithmetic and copies ran while one was open for 1% of the time, Pallas kernels for 0%

profile of v1, /device:TPU:0, one launch (start us, length us, event | category | flops | bytes accessed | tf_op | source)
XLA Modules:
  0.0 163.6 jit_solution(7518645076740975425)
XLA Ops:
  6.5 0.0 all-reduce.4.cloned.1.call-start
  6.5 1.4 fusion.65
  10.4 3.3 %broadcast_select_fusion.3 = (bf16[256,2048]{1,0:T(8,128)(2,1)}, bf16[256,2048]{1,0:T(8,128)(2,1)}, bf16[256,2048]{1,0:T(8,128)(2,1)}, bf16[256,2048]{1,0:T(8,128)(2,1)}) fusion(bf16[256,2048]{1,0:T(8,128)(2,1)} %param.7, pred[]{:T(512)S(6)} %eq.19, pred[]{:T(512)S(6)} %eq.20, pred[]{:T(512)S(6)} %eq.22, pred[]{:T(512)S(6)} %eq.21), kind=kLoop, calls=%fused_computation.117 | loop fusion | flops 2097152 | bytes 5242884 | tf_op jit(solution)/shard_map/jit(_where)/select_n | solution.py:14
  13.8 0.0 copy-start.5
  13.8 0.0 all-reduce.4.cloned.1.call-update
  13.8 1.0 copy-done.5
  14.8 0.0 copy-start.3
  14.8 0.3 copy.19
  15.2 0.9 copy-done.3
  16.0 0.5 fusion.15
  16.5 0.0 copy-start
  16.6 16.0 %all-reduce = (f32[256]{0:T(256)S(1)}, f32[256]{0:T(256)S(1)}, f32[256]{0:T(256)S(1)}, f32[256]{0:T(256)S(1)}) all-reduce(f32[256]{0:T(256)S(1)} %get-tuple-element.29, f32[256]{0:T(256)S(1)} %get-tuple-element.28, f32[256]{0:T(256)S(1)} %get-tuple-element.27, ...), channel_id=1, replica_groups=mesh['field'=8,'point'=4] {'field'}, use_global_device_ids=true, to_apply=%region_1.2 | all-reduce | flops 1024 | bytes 8192 | tf_op jit(solution)/shard_map/psum | solution.py:15
  32.6 0.1 bitcast_convert_fusion
  32.7 65.1 %all-reduce.4.cloned.1.call-done = (bf16[256,2048]{1,0:T(8,128)(2,1)}, bf16[256,2048]{1,0:T(8,128)(2,1)}, bf16[256,2048]{1,0:T(8,128)(2,1)}, bf16[256,2048]{1,0:T(8,128)(2,1)}) async-done(((bf16[256,2048]{1,0:T(8,128)(2,1)}, bf16[256,2048]{1,0:T(8,128)(2,1)}, bf16[256,2048]{1,0:T(8,128)(2,1)}, bf16[256,2048]{1,0:T(8,128)(2,1)}), (bf16[256,2048]{1,0:T(8,128)(2,1)}, bf16[256,2048]{1,0:T(8,128)(2,1)}, ...) | async-done | bytes 4194320 | tf_op jit(solution)/shard_map/psum | solution.py:15
  97.8 0.0 copy-done
  97.8 0.0 copy-start.2
  97.8 1.8 %fusion.14 = f32[256,256]{0,1:T(8,128)S(1)} fusion(bf16[256,2048]{1,0:T(8,128)(2,1)} %get-tuple-element.12, bf16[1,256,2048]{2,1,0:T(8,128)(2,1)S(1)} %copy-done, f32[256,4,256]{0,2,1:T(8,128)S(1)} %bitcast_convert_fusion, f32[256]{0:T(256)S(1)} %get-tuple-element.5), kind=kOutput, calls=%fused_computation.37 | convolution fusion | flops 268632064 | bytes 2622464 | tf_op jit(solution)/shard_map/dot_general | solution.py:70
  99.6 0.0 copy-done.2
  99.6 0.0 copy-start.1
  99.6 0.5 fusion
  100.0 0.7 copy-done.1
  100.8 0.5 fusion.11
  101.3 0.0 copy-start.4
  101.3 0.5 fusion.1
  101.8 0.7 copy-done.4
  102.5 0.5 fusion.9
  103.0 2.5 %fusion.7 = f32[256,1,256]{0,2,1:T(8,128)S(1)} fusion(bf16[256,2048]{1,0:T(8,128)(2,1)} %get-tuple-element.9, bf16[256,2048]{1,0:T(8,128)(2,1)} %get-tuple-element.10, bf16[256,2048]{1,0:T(8,128)(2,1)S(1)} %fusion.1, f32[256,4,256]{0,2,1:T(8,128)S(1)} %bitcast_convert_fusion, f32[256,256]{0,1:T(8,128)S(1)} %fusion.9, f32[256]{0:T(256)S(1)} %get-tuple-element.8), kind=kOutput, calls=%fused_computation.27 | convolution fusion | flops 538771456 | bytes 4195328 | tf_op jit(solution)/shard_map/dot_general | solution.py:70
  105.5 0.1 pad_maximum_fusion.24
  105.6 1.6 %copy.23 = f32[256,4,256]{0,1,2:T(4,128)} copy(f32[256,4,256]{0,2,1:T(8,128)S(1)} %pad_maximum_fusion.24) | data formatting | bytes 2097152 | tf_op jit(solution)/shard_map/stack | solution.py:82
  107.2 4.7 %all-to-all-start = ((f32[256,4,256]{0,1,2:T(4,128)}), f32[256,4,256]{0,1,2:T(4,128)S(1)}, u32[]{:S(2)}, u32[]{:S(2)}) async-start(f32[256,4,256]{0,1,2:T(4,128)} %copy.23), calls=%async_computation | async-start | bytes 2097152 | tf_op jit(solution)/shard_map/all_to_all | solution.py:84
  111.9 0.0 copy-done.6
  111.9 2.0 %collective-permute-start = (s32[256]{0:T(256)S(1)}, s32[256]{0:T(256)S(1)}, u32[]{:S(2)}, u32[]{:S(2)}) collective-permute-start(s32[256]{0:T(256)S(1)} %bitcast.77), channel_id=1, source_target_pairs={{0,1},{1,2},{2,3},{3,0},{4,5},{5,6},{6,7},{7,4},{8,9},{9,10},{10,1... | collective-permute-start | bytes 3080 | tf_op jit(solution)/shard_map/ppermute | solution.py:60
  114.0 18.9 %collective-permute-done = s32[256]{0:T(256)S(1)} collective-permute-done((s32[256]{0:T(256)S(1)}, s32[256]{0:T(256)S(1)}, u32[]{:S(2)}, u32[]{:S(2)}) %collective-permute-start) | collective-permute-done | bytes 1056 | tf_op jit(solution)/shard_map/ppermute | solution.py:60
  132.9 3.3 %collective-permute-start.1 = (s32[256]{0:T(256)S(1)}, s32[256]{0:T(256)S(1)}, u32[]{:S(2)}, u32[]{:S(2)}) collective-permute-start(s32[256]{0:T(256)S(1)} %collective-permute-done), channel_id=1, source_target_pairs={{0,1},{1,2},{2,3},{3,0},{4,5},{5,6},{6,7},{7,4},{8,9},{9,10},{10,1... | collective-permute-start | bytes 3080 | tf_op jit(solution)/shard_map/ppermute | solution.py:60
  136.2 2.1 %collective-permute-done.1 = s32[256]{0:T(256)S(1)} collective-permute-done((s32[256]{0:T(256)S(1)}, s32[256]{0:T(256)S(1)}, u32[]{:S(2)}, u32[]{:S(2)}) %collective-permute-start.1) | collective-permute-done | bytes 1056 | tf_op jit(solution)/shard_map/ppermute | solution.py:60
  138.2 1.6 collective-permute-start.2
  139.9 3.7 %collective-permute-done.2 = s32[256]{0:T(256)S(1)} collective-permute-done((s32[256]{0:T(256)S(1)}, s32[256]{0:T(256)S(1)}, u32[]{:S(2)}, u32[]{:S(2)}) %collective-permute-start.2) | collective-permute-done | bytes 1056 | tf_op jit(solution)/shard_map/ppermute | solution.py:60
  143.7 0.1 compare_select_fusion
  143.8 0.0 all-to-all-done
  143.8 0.7 copy.24
  144.5 0.2 copy.30
  144.7 0.3 copy.25
  145.0 5.2 %scatter_custom_fusion = f32[256,1024]{0,1:T(8,128)S(1)} fusion(s32[1024]{0:T(1024)S(1)} %compare_select_fusion, f32[1024,256]{1,0:T(8,128)S(1)} %copy.25, f32[]{:T(128)} %constant.54.clone.1), kind=kCustom, calls=%fused_computation.119 | custom fusion | bytes 1048580 | tf_op jit(solution)/shard_map/scatter | solution.py:47
  150.3 1.3 multiply_add_fusion.3
  151.6 1.3 multiply_add_fusion.2
  152.9 1.3 multiply_add_fusion.1
  154.2 1.3 multiply_add_fusion
  155.5 1.3 copy.26
  (16 shorter events, 0.1 us)
Async XLA Ops:
  6.5 91.2 %all-reduce.4.cloned.1.call-start = ((), (), s32[]{:S(2)}) async-start(), calls=%async_computation.1 | async-start | bytes 8388608 | tf_op jit(solution)/shard_map/psum | solution.py:15
  13.8 1.0 copy-start.5
  14.8 1.2 copy-start.3
  16.5 81.2 %copy-start = (bf16[1,256,2048]{2,1,0:T(8,128)(2,1)S(1)}, bf16[1,256,2048]{2,1,0:T(8,128)(2,1)}, u32[]{:S(2)}) copy-start(bf16[1,256,2048]{2,1,0:T(8,128)(2,1)} %param.5) | copy-start | bytes 3145732
  97.8 1.8 %copy-start.2 = (bf16[256,2048]{1,0:T(8,128)(2,1)S(1)}, bf16[256,2048]{1,0:T(8,128)(2,1)}, u32[]{:S(2)}) copy-start(bf16[256,2048]{1,0:T(8,128)(2,1)} %get-tuple-element.12) | copy-start | bytes 3145732
  99.6 1.2 copy-start.1
  101.3 1.2 copy-start.4
  107.2 4.7 %copy-start.6 = (s32[1,256]{1,0:T(1,128)S(1)}, s32[1,256]{1,0:T(1,128)}, u32[]{:S(2)}) copy-start(s32[1,256]{1,0:T(1,128)} %param.9) | copy-start | bytes 3076
  107.2 36.6 %all-to-all-start = ((f32[256,4,256]{0,1,2:T(4,128)}), f32[256,4,256]{0,1,2:T(4,128)S(1)}, u32[]{:S(2)}, u32[]{:S(2)}) async-start(f32[256,4,256]{0,1,2:T(4,128)} %copy.23), calls=%async_computation | async-start | bytes 2097152 | tf_op jit(solution)/shard_map/all_to_all | solution.py:84
  111.9 20.9 %collective-permute-start = (s32[256]{0:T(256)S(1)}, s32[256]{0:T(256)S(1)}, u32[]{:S(2)}, u32[]{:S(2)}) collective-permute-start(s32[256]{0:T(256)S(1)} %bitcast.77), channel_id=1, source_target_pairs={{0,1},{1,2},{2,3},{3,0},{4,5},{5,6},{6,7},{7,4},{8,9},{9,10},{10,1... | collective-permute-start | bytes 3080 | tf_op jit(solution)/shard_map/ppermute | solution.py:60
  132.9 5.4 %collective-permute-start.1 = (s32[256]{0:T(256)S(1)}, s32[256]{0:T(256)S(1)}, u32[]{:S(2)}, u32[]{:S(2)}) collective-permute-start(s32[256]{0:T(256)S(1)} %collective-permute-done), channel_id=1, source_target_pairs={{0,1},{1,2},{2,3},{3,0},{4,5},{5,6},{6,7},{7,4},{8,9},{9,10},{10,1... | collective-permute-start | bytes 3080 | tf_op jit(solution)/shard_map/ppermute | solution.py:60
  138.2 5.4 %collective-permute-start.2 = (s32[256]{0:T(256)S(1)}, s32[256]{0:T(256)S(1)}, u32[]{:S(2)}, u32[]{:S(2)}) collective-permute-start(s32[256]{0:T(256)S(1)} %collective-permute-done.1), channel_id=1, source_target_pairs={{0,1},{1,2},{2,3},{3,0},{4,5},{5,6},{6,7},{7,4},{8,9},{9,10},{10,1... | collective-permute-start | bytes 3080 | tf_op jit(solution)/shard_map/ppermute | solution.py:60
Sparse Core Ops, SparseCore 0:
  13.9 83.7 all-reduce.3
